TPU v7x, 32 devices: a whole 2x2x4 slice. The times are simulated.
32 devices in a mesh: dp: 8 (over z, y), tm: 4 (over x, core).
Axes of the slice: x: 2, y: 2, z: 4, core: 2. Of those that a mesh axis runs over, the one named last changes fastest.
Arguments:
- latents: bfloat16 [8, 16, 16, 16, 640], P('dp', 'tm'), may hold values from -60 to 60
- cotangent: bfloat16 [8, 8, 16, 16, 640], P('dp', 'tm'), may hold values from -6 to 6
- timesteps: int32 [8], P('dp'), may hold values from 0 to 999
- spatial_weight: bfloat16 [640, 5760], P('dp'), may hold values from -0.078125 to 0.078125
- temporal_weight: bfloat16 [640, 1920], P('dp'), may hold values from -0.125 to 0.125
- time_weight: bfloat16 [640, 256], P('dp'), may hold values from -0.375 to 0.375
Outputs:
- downsampled: float32 [8, 8, 16, 16, 640], P('dp', 'tm')
- latents_grad: float32 [8, 16, 16, 16, 640], P('dp', 'tm')
- spatial_grad: float32 [640, 5760], P('dp')
- temporal_grad: float32 [640, 1920], P('dp')
- time_grad: float32 [640, 256], P('dp')
All inputs are finite; a program needn't handle non-finite values.
Results may differ from a plain program's by a relative error of at most 0.0041.
Values may be sent and summed in bfloat16 or wider, within the bound.
No kernel may reach another device: no remote copies, remote signals or barrier semaphores. Data moves between devices by JAX's collectives and lax.ppermute only.
A program may use at most 128 MiB of HBM per device.

v0:
```python
import math
import jax
import jax.numpy as jnp
from jax import lax
from jax.sharding import PartitionSpec as P

GROUPS = 32
epsilon = 1e-05
log_base = math.log(10000.0)


def from_behind(x, axis, by):
    count = lax.axis_size(axis)
    pairs = [(i, i + by) for i in range(count) if 0 <= i + by < count]
    return lax.ppermute(x, axis, pairs)


def embedding(diffusion_step, embed_width):
    half_width = embed_width // 2
    frequency = jnp.exp(-log_base * jnp.arange(half_width, dtype=jnp.float32) / half_width)
    angles = diffusion_step.astype(jnp.float32) * frequency
    return jnp.concatenate([jnp.cos(angles), jnp.sin(angles)])


def normalize(frames):
    frame_count, height, breadth, channels = frames.shape
    grouped = frames.astype(jnp.float32).reshape(
        frame_count, height * breadth, GROUPS, channels // GROUPS
    )
    center = jnp.mean(grouped, axis=(1, 3), keepdims=True)
    deviation = grouped - center
    variance = jnp.mean(deviation * deviation, axis=(1, 3), keepdims=True)
    scaled = lax.rsqrt(variance + epsilon)
    return (deviation * scaled, scaled)


def spatial_columns(activation):
    frame_count, height, breadth, channels = activation.shape
    padded = jnp.pad(activation, ((0, 0), (1, 1), (1, 1), (0, 0)))
    shifted_views = [
        padded[:, row_shift : row_shift + height, col_shift : col_shift + breadth, :]
        for row_shift in range(3)
        for col_shift in range(3)
    ]
    return jnp.stack(shifted_views, axis=3).reshape(frame_count * height * breadth, 9, channels)


def spatial_fold(pieces, frame_count, height, breadth):
    channels = pieces.shape[-1]
    layout = pieces.reshape(frame_count, height, breadth, 9, channels)
    total = jnp.zeros((frame_count, height + 2, breadth + 2, channels), jnp.float32)
    for row_shift in range(3):
        for col_shift in range(3):
            placed = jnp.pad(
                layout[:, :, :, 3 * row_shift + col_shift, :],
                ((0, 0), (row_shift, 2 - row_shift), (col_shift, 2 - col_shift), (0, 0)),
            )
            total = total + placed
    return total[:, 1 : height + 1, 1 : breadth + 1, :]


def temporal_columns(extended):
    out_count = (extended.shape[0] - 1) // 2
    taps = [extended[offset : offset + 2 * out_count : 2] for offset in range(3)]
    return jnp.stack(taps, axis=2).reshape(out_count * extended.shape[1], 3, extended.shape[2])


def temporal_back(parts, incoming):
    lead_tap = parts[:, :, 0, :]
    mid_tap = parts[:, :, 1, :]
    tail_tap = parts[:, :, 2, :]
    even_frames = jnp.concatenate([lead_tap[1:], incoming[None]], axis=0) + tail_tap
    merged = jnp.stack([mid_tap, even_frames], axis=1)
    return (merged.reshape(2 * parts.shape[0], parts.shape[1], parts.shape[3]), lead_tap[0])


def spatial_forward(frames, spatial_taps, time_shift):
    frame_count, height, breadth, channels = frames.shape
    normal, scaled = normalize(frames)
    activation = (
        jax.nn.silu(normal).reshape(frame_count, height, breadth, channels).astype(jnp.bfloat16)
    )
    columns = spatial_columns(activation)
    conv_sum = (
        jnp.einsum("rkc,ckq->rq", columns, spatial_taps, preferred_element_type=jnp.float32)
        + time_shift
    )
    hidden = conv_sum.astype(jnp.bfloat16).reshape(frame_count, height * breadth, channels)
    return (hidden, normal, scaled, columns)


def body(latents, cotangent, timesteps, spatial_weight, temporal_weight, time_weight):
    clip_frames = latents[0]
    frame_count, height, breadth, channels = clip_frames.shape
    pixels = height * breadth
    out_count = frame_count // 2
    spatial_full, temporal_full, time_full = (
        lax.all_gather(spatial_weight, "dp", axis=0, tiled=True),
        lax.all_gather(temporal_weight, "dp", axis=0, tiled=True),
        lax.all_gather(time_weight, "dp", axis=0, tiled=True),
    )
    spatial_taps = spatial_full.reshape(channels, 9, channels)
    temporal_taps = temporal_full.reshape(channels, 3, channels)
    embedded = embedding(timesteps[0], time_full.shape[1])
    time_shift = jnp.dot(time_full.astype(jnp.float32), embedded, precision=lax.Precision.HIGHEST)
    hidden, normal, scaled, columns = spatial_forward(clip_frames, spatial_taps, time_shift)
    before = from_behind(hidden[-1], "tm", 1)
    extended = jnp.concatenate([before[None], hidden], axis=0)
    tcols = temporal_columns(extended)
    result = jnp.einsum("rkc,ckq->rq", tcols, temporal_taps, preferred_element_type=jnp.float32)
    downsampled = result.reshape(1, out_count, height, breadth, channels)
    grad_out = cotangent[0].reshape(out_count * pixels, channels)
    parts = jnp.einsum(
        "rq,ckq->rkc", grad_out, temporal_taps, preferred_element_type=jnp.float32
    ).reshape(out_count, pixels, 3, channels)
    local_grad, leaving = temporal_back(parts, jnp.zeros((pixels, channels), jnp.float32))
    arriving = from_behind(leaving, "tm", -1)
    hidden_grad = local_grad.at[-1].add(arriving)
    hidden_back = hidden_grad.astype(jnp.bfloat16).reshape(frame_count * pixels, channels)
    shift_grad = jnp.sum(hidden_grad, axis=(0, 1))
    pieces = jnp.einsum(
        "rq,ckq->rkc", hidden_back, spatial_taps, preferred_element_type=jnp.float32
    )
    activation_grad = spatial_fold(pieces, frame_count, height, breadth)
    sigmoid_value = jax.nn.sigmoid(normal)
    derivative = sigmoid_value * (1.0 + normal * (1.0 - sigmoid_value))
    norm_grad = activation_grad.reshape(normal.shape) * derivative
    mean_one = jnp.mean(norm_grad, axis=(1, 3), keepdims=True)
    mean_two = jnp.mean(norm_grad * normal, axis=(1, 3), keepdims=True)
    input_grad = ((norm_grad - mean_one - normal * mean_two) * scaled).reshape(
        1, frame_count, height, breadth, channels
    )
    row_share = channels // lax.axis_size("dp")
    spatial_part = jnp.einsum(
        "rkc,rq->ckq", columns, hidden_back, preferred_element_type=jnp.float32
    )
    temporal_part = jnp.einsum("rkc,rq->ckq", tcols, grad_out, preferred_element_type=jnp.float32)
    time_part = shift_grad[:, None] * embedded[None, :]
    grad_shard = lax.psum_scatter(
        jnp.concatenate(
            [
                spatial_part.reshape(row_share * lax.axis_size("dp"), 9 * channels),
                temporal_part.reshape(row_share * lax.axis_size("dp"), 3 * channels),
                time_part,
            ],
            axis=1,
        ),
        "dp",
        scatter_dimension=0,
        tiled=True,
    )
    totals = lax.psum(grad_shard, "tm")
    spatial_grad = totals[:, : 9 * channels]
    temporal_grad = totals[:, 9 * channels : 12 * channels]
    time_grad = totals[:, 12 * channels :]
    return (downsampled, input_grad, spatial_grad, temporal_grad, time_grad)


def solution(mesh):
    placed = (
        P("dp", "tm", None, None, None),
        P("dp", "tm", None, None, None),
        P("dp"),
        P("dp", None),
        P("dp", None),
        P("dp", None),
    )
    return jax.shard_map(
        body,
        mesh=mesh,
        in_specs=placed,
        out_specs=(
            P("dp", "tm", None, None, None),
            P("dp", "tm", None, None, None),
            P("dp", None),
            P("dp", None),
            P("dp", None),
        ),
        check_vma=False,
    )
```

profile of v0, /device:TPU:0, one launch (start us, length us, event | category | flops | bytes accessed | tf_op | source)
XLA Modules:
  0.0 723.6 jit_solution(1900016296076289256)
XLA Ops:
  7.2 0.7 all-gather.5.cloned.1.call-update
  8.0 0.7 all-gather.3.cloned.1.call-update
  8.7 1.5 convert_reduce_fusion
  10.7 0.4 multiply_reduce_fusion.1
  12.2 33.4 %all_gather.10 = bf16[640,256]{1,0:T(8,128)(2,1)S(1)} all-gather(bf16[80,256]{1,0:T(8,128)(2,1)S(1)} %copy-done.14), channel_id=1, replica_groups=mesh['dp'=8,'tm'=4] {'dp'}, dimensions={0}, use_global_device_ids=true | all-gather | bytes 368640 | tf_op jit(solution)/shard_map/all_gather | solution.py:100
  45.6 0.4 convolution_reduce_fusion
  46.0 20.7 %all-gather.5.cloned.1.call-done = bf16[640,1920]{1,0:T(8,128)(2,1)} async-done(((bf16[80,1920]{1,0:T(8,128)(2,1)}), bf16[640,1920]{1,0:T(8,128)(2,1)}) %all-gather.5.cloned.1.call-update) | async-done | bytes 2457616 | tf_op jit(solution)/shard_map/all_gather | solution.py:99
  66.7 4.3 copy.34
  71.0 3.4 fusion.18
  74.5 1.5 collective-permute-start.1
  76.6 1.9 collective-permute-done.1
  78.7 0.3 fusion.13
  79.0 1.2 broadcast_multiply_fusion
  80.2 100.1 %all-gather.3.cloned.1.call-done = bf16[640,5760]{1,0:T(8,128)(2,1)} async-done(((bf16[80,5760]{1,0:T(8,128)(2,1)}), bf16[640,5760]{1,0:T(8,128)(2,1)}) %all-gather.3.cloned.1.call-update) | async-done | bytes 7372816 | tf_op jit(solution)/shard_map/all_gather | solution.py:98
  180.3 10.3 %copy.32 = bf16[640,5760]{0,1:T(8,128)(2,1)} copy(bf16[640,5760]{1,0:T(8,128)(2,1)} %all-gather.3.cloned.1.call-done) | data formatting | bytes 14745600 | tf_op jit(solution)/shard_map/all_gather | solution.py:98
  190.6 15.7 %fusion.16 = f32[1024,640,9]{1,0,2:T(8,128)} fusion(bf16[1024,640,1]{1,0,2:T(8,128)(2,1)S(1)} %bitcast.165, bf16[640,9,640]{0,2,1:T(8,128)(2,1)} %bitcast.137), kind=kOutput, calls=%fused_computation.78 | convolution fusion | flops 7549747200 | bytes 32276480 | tf_op jit(solution)/shard_map/rq,ckq->rkc/dot_general | solution.py:121
  206.2 13.8 %slice_bitcast_fusion.8 = (f32[4,16,16,640]{3,2,1,0:T(8,128)}, f32[4,16,16,640]{3,2,1,0:T(8,128)S(1)}, f32[4,16,16,640]{3,2,1,0:T(8,128)S(1)}, f32[4,16,16,640]{...) fusion(f32[4,16,16,9,640]{4,2,1,0,3:T(8,128)} %bitcast.132), kind=kLoop, calls=%fused_computation.24 | loop fusion | bytes 47185920 | tf_op jit(solution)/shard_map/squeeze | solution.py:55
  220.1 4.2 pad_add_fusion
  224.3 0.6 copy-done.3
  224.9 0.8 copy-done.4
  225.7 3.8 multiply_multiply_fusion
  229.4 1.0 fusion.12
  230.5 3.0 pad_slice_fusion
  234.7 0.8 constant_dynamic-update-slice_fusion.4
  235.6 4.4 copy-done.13
  239.9 1.2 constant_dynamic-update-slice_fusion.3
  241.1 1.2 constant_dynamic-update-slice_fusion.2
  242.3 1.2 constant_dynamic-update-slice_fusion.1
  243.5 1.2 constant_dynamic-update-slice_fusion
  244.6 12.7 %fusion.3 = bf16[1024,640]{1,0:T(8,128)(2,1)S(1)} fusion(bf16[1024,9,640]{2,0,1:T(8,128)(2,1)} %constant_dynamic-update-slice_fusion, bf16[640,9,640]{0,2,1:T(8,128)(2,1)S(1)} %bitcast.140, f32[640]{0:T(1024)S(1)} %convolution_reduce_fusion), kind=kOutput, calls=%fused_computation.31 | convolution fusion | flops 7551057920 | bytes 20482560 | tf_op jit(solution)/shard_map/rkc,ckq->rq/dot_general | solution.py:85
  257.4 0.8 slice.149
  258.1 2.1 collective-permute-start
  260.2 15.0 %fusion.17 = f32[640,9,640]{2,0,1:T(8,128)} fusion(bf16[1024,640,1]{1,0,2:T(8,128)(2,1)S(1)} %bitcast.166, bf16[1024,9,640]{2,0,1:T(8,128)(2,1)} %constant_dynamic-update-slice_fusion), kind=kOutput, calls=%fused_computation.79 | convolution fusion | flops 7549747200 | bytes 27852800 | tf_op jit(solution)/shard_map/rkc,rq->ckq/dot_general | solution.py:134
  275.2 15.1 %copy.44 = f32[640,5760]{1,0:T(8,128)} copy(f32[640,5760]{0,1:T(8,128)} %bitcast.133) | data formatting | bytes 29491200 | tf_op jit(solution)/shard_map/reshape | solution.py:142
  290.5 1.4 pad_maximum_fusion.3
  291.9 3.9 fusion.11
  295.8 6.0 copy.45
  301.8 15.2 %pad_maximum_fusion = f32[640,7936]{1,0:T(8,128)} fusion(f32[640,256]{1,0:T(8,128)S(1)} %copy-done.9, f32[640,1920]{1,0:T(8,128)} %copy.45, f32[640,5760]{1,0:T(8,128)} %copy.44), kind=kLoop, calls=%fused_computation | loop fusion | flops 10158080 | bytes 40632320 | tf_op jit(solution)/shard_map/concatenate | solution.py:140
  317.9 332.6 %reduce-scatter.2.cloned.1.call-done = f32[80,7936]{1,0:T(8,128)} async-done(((f32[640,7936]{1,0:T(8,128)}), f32[80,7936]{1,0:T(8,128)}) %reduce-scatter.2.cloned.1.call-update) | async-done | bytes 2539536 | tf_op jit(solution)/shard_map/reduce_scatter | solution.py:139
  650.5 4.7 fusion.2
  655.3 0.3 pad_maximum_fusion.2
  655.5 1.4 copy-done.10
  656.9 1.8 fusion.15
  658.9 1.1 copy.46
  660.0 50.8 %all-reduce.13.cloned.1.call-done = f32[80,7936]{1,0:T(8,128)} async-done(((f32[80,7936]{1,0:T(8,128)}), f32[80,7936]{1,0:T(8,128)}) %all-reduce.13.cloned.1.call-update) | async-done | bytes 2539536 | tf_op jit(solution)/shard_map/psum | solution.py:152
  710.8 2.9 slice.165
  713.6 1.9 slice.166
  715.6 1.5 slice.167
  (75 shorter events, 4.2 us)
Async XLA Ops:
  7.2 63.8 %copy-start = (bf16[1,2,16,16,640]{4,3,2,1,0:T(8,128)(2,1)S(1)}, bf16[1,2,16,16,640]{4,3,2,1,0:T(8,128)(2,1)}, u32[]{:S(2)}) copy-start(bf16[1,2,16,16,640]{4,3,2,1,0:T(8,128)(2,1)} %param.9) | copy-start | bytes 1966084
  7.2 3.5 copy-start.1
  7.2 5.0 copy-start.14
  7.2 59.5 %all-gather.5.cloned.1.call-start = ((), (), s32[]{:S(2)}) async-start(), calls=%async_computation.2 | async-start | bytes 2764800 | tf_op jit(solution)/shard_map/all_gather | solution.py:99
  7.9 172.4 %all-gather.3.cloned.1.call-start = ((), (), s32[]{:S(2)}) async-start(), calls=%async_computation.1 | async-start | bytes 8294400 | tf_op jit(solution)/shard_map/all_gather | solution.py:98
  8.7 641.8 %reduce-scatter.2.cloned.1.call-start = ((), (), s32[]{:S(2)}) async-start(), calls=%async_computation.3 | async-start | bytes 22855680 | tf_op jit(solution)/shard_map/reduce_scatter | solution.py:139
  74.5 4.0 collective-permute-start.1
  79.0 111.6 %copy-start.11 = (bf16[4,256,640]{2,1,0:T(8,128)(2,1)}, bf16[4,256,640]{2,1,0:T(8,128)(2,1)S(1)}, u32[]{:S(2)}) copy-start(bf16[4,256,640]{2,1,0:T(8,128)(2,1)S(1)} %get-tuple-element.38) | copy-start | bytes 3932164
  220.0 4.3 copy-start.2
  220.0 4.8 copy-start.3
  220.0 5.6 copy-start.4
  234.7 9.9 %slice-start = ((s8[7372800]{0:T(1024)(128)(4,1)}), s8[4194304]{0:T(1024)(128)(4,1)S(1)}, s32[]{:S(2)}) async-start(s8[7372800]{0:T(1024)(128)(4,1)} %bitcast.138), calls=%async_computation.5 | async-start | bytes 8388608
  235.6 4.4 copy-start.13
  239.9 4.7 slice-start.1
  244.6 15.6 %copy-start.12 = (bf16[4,256,640]{2,1,0:T(8,128)(2,1)S(1)}, bf16[4,256,640]{2,1,0:T(8,128)(2,1)}, u32[]{:S(2)}) copy-start(bf16[4,256,640]{2,1,0:T(8,128)(2,1)} %copy-done.11) | copy-start | bytes 3932164
  258.1 32.3 %collective-permute-start = (bf16[256,640]{1,0:T(8,128)(2,1)}, bf16[256,640]{1,0:T(8,128)(2,1)}, u32[]{:S(2)}, u32[]{:S(2)}) collective-permute-start(bf16[256,640]{1,0:T(8,128)(2,1)} %slice.149), channel_id=1, source_target_pairs={{0,1},{1,2},{2,3},{4,5},{5,6},{6,7},{8,9},{9,10},{10,11},{12,13},{... | collective-permute-start | bytes 983048 | tf_op jit(solution)/shard_map/ppermute | solution.py:15
  290.4 5.4 copy-start.5
  290.5 5.4 copy-start.7
  295.8 6.0 copy-start.9
  317.0 393.8 %all-reduce.13.cloned.1.call-start = ((), (), s32[]{:S(2)}) async-start(), calls=%async_computation.4 | async-start | bytes 5079040 | tf_op jit(solution)/shard_map/psum | solution.py:152
  650.5 4.7 copy-start.6
  650.5 4.7 copy-start.8
  655.3 1.7 copy-start.10
Sparse Core Ops, SparseCore 0:
  10.2 56.4 all-gather.4
  68.9 111.3 all-gather.2
  317.1 333.2 reduce-scatter.1
  652.9 57.8 all-reduce.12
where the time goes:
time: 725 us; the launch traced here: 724 us
  waiting for transfers between devices  508 us (70%)
  local copies, waits for them, and re-layouts  75.6 us (10%)
  matrix products  52.9 us (7%)
  other arithmetic  35.7 us (5%)
  blocking collectives  33.4 us (5%)
  between operations  14.9 us (2%)
    reduce_scatter x1, waiting for transfers between devices, body(): lax.psum_scatter(jnp.concatenate([spatial_part.reshape(row_share * lax.ax...  333 us
    all_gather x1, waiting for transfers between devices, body(): lax.all_gather(spatial_weight, 'dp', axis=0, tiled=True)  100 us
    psum x1, waiting for transfers between devices, body(): totals = lax.psum(grad_shard, 'tm')  50.8 us
    all_gather x1, blocking collectives, body(): lax.all_gather(time_weight, 'dp', axis=0, tiled=True)  33.4 us
    all_gather x1, waiting for transfers between devices, body(): lax.all_gather(temporal_weight, 'dp', axis=0, tiled=True)  20.7 us
    dot_general x1, matrix products, body(): jnp.einsum('rq,ckq->rkc', hidden_back, spatial_taps, preferred_element_ty...  15.7 us
    concatenate x1, other arithmetic, body(): jnp.concatenate([spatial_part.reshape(row_share * lax.axis_size('dp'), 9...  15.2 us
    reshape x1, local copies, waits for them, and re-layouts, body(): spatial_part.reshape(row_share * lax.axis_size('dp'), 9 * channels)  15.1 us
  transfers between devices with their start and end apart: 6, of which 5 were waited for; matrix products, arithmetic and copies ran while one was open for 7% of the time, Pallas kernels for 0%

commit v1 on v0

--- a/solution.py
+++ b/solution.py
@@ -7,6 +7,27 @@
 GROUPS = 32
 epsilon = 1e-05
 log_base = math.log(10000.0)
+
+
+def laid_out(blocks, dim):
+    blocks = jnp.moveaxis(blocks, 0, dim)
+    shape = blocks.shape
+    return blocks.reshape(*shape[:dim], shape[dim] * shape[dim + 1], *shape[dim + 2 :])
+
+
+def collected_by_bits(x, axis):
+    count, position = (lax.axis_size(axis), lax.axis_index(axis))
+    blocks, stride = (x[None], 1)
+    while stride < count:
+        other = lax.ppermute(blocks, axis, [(i, i ^ stride) for i in range(count)])
+        low = position & stride == 0
+        blocks = jnp.concatenate([jnp.where(low, blocks, other), jnp.where(low, other, blocks)])
+        stride *= 2
+    return blocks
+
+
+def doubled_up(x, axis, dim):
+    return laid_out(collected_by_bits(x, axis), dim)
 
 
 def from_behind(x, axis, by):
@@ -96,7 +117,7 @@
     out_count = frame_count // 2
     spatial_full, temporal_full, time_full = (
         lax.all_gather(spatial_weight, "dp", axis=0, tiled=True),
-        lax.all_gather(temporal_weight, "dp", axis=0, tiled=True),
+        doubled_up(temporal_weight, "dp", 0),
         lax.all_gather(time_weight, "dp", axis=0, tiled=True),
     )
     spatial_taps = spatial_full.reshape(channels, 9, channels)

time: 725 us -> 768 us (1.059)
  blocking collectives: 33.4 us -> 127 us
  waiting for transfers between devices: 508 us -> 433 us
  starting transfers between devices: 3.69 us -> 18.9 us
    all_gather x1, waiting for transfers between devices: 100 us -> 0.01 us  [body(): lax.all_gather(spatial_weight, 'dp', axis=0, tiled=True)]
    all_gather x1, blocking collectives: 33.4 us -> 127 us  [body(): lax.all_gather(time_weight, 'dp', axis=0, tiled=True)]
    ppermute x0 -> x3, waiting for transfers between devices: none -> 48.4 us  [collected_by_bits(): other = lax.ppermute(blocks, axis, [(i, i ^ stride) for i in range(count)])]
    all_gather x1 -> x0, waiting for transfers between devices: 20.7 us -> none  [body(): lax.all_gather(temporal_weight, 'dp', axis=0, tiled=True)]
    ppermute x2, starting transfers between devices: 3.53 us -> 11.9 us  [from_behind(): return lax.ppermute(x, axis, pairs)]
  transfers between devices with their start and end apart: 6 -> 8, of which waited for: 5 -> 5; matrix products, arithmetic and copies ran while one was open for 7% -> 8% of each run, Pallas kernels for 0% -> 0%
where the time goes in v1:
time: 768 us; the launch traced here: 767 us
  waiting for transfers between devices  433 us (56%)
  blocking collectives  127 us (17%)
  local copies, waits for them, and re-layouts  78.5 us (10%)
  matrix products  53.1 us (7%)
  other arithmetic  41.2 us (5%)
  starting transfers between devices  18.9 us (2%)
  between operations  14.8 us (2%)
    reduce_scatter x1, waiting for transfers between devices, body(): lax.psum_scatter(jnp.concatenate([spatial_part.reshape(row_share * lax.ax...  331 us
    all_gather x1, blocking collectives, body(): lax.all_gather(time_weight, 'dp', axis=0, tiled=True)  127 us
    psum x1, waiting for transfers between devices, body(): totals = lax.psum(grad_shard, 'tm')  50.7 us
    ppermute x3, waiting for transfers between devices, collected_by_bits(): other = lax.ppermute(blocks, axis, [(i, i ^ stride) for i in range(count)])  48.4 us
    dot_general x1, matrix products, body(): jnp.einsum('rq,ckq->rkc', hidden_back, spatial_taps, preferred_element_ty...  15.7 us
  transfers between devices with their start and end apart: 8, of which 5 were waited for; matrix products, arithmetic and copies ran while one was open for 8% of the time, Pallas kernels for 0%

profile of v1, /device:TPU:0, one launch (start us, length us, event | category | flops | bytes accessed | tf_op | source)
XLA Modules:
  0.0 766.8 jit_solution(15085166565373267573)
XLA Ops:
  8.0 3.0 collective-permute-start.1
  11.0 7.5 collective-permute-done.1
  18.5 1.0 broadcast_select_fusion.5
  20.3 1.9 collective-permute-start.2
  22.2 40.9 %collective-permute-done.2 = bf16[2,80,1920]{2,1,0:T(8,128)(2,1)} collective-permute-done((bf16[2,80,1920]{2,1,0:T(8,128)(2,1)S(1)}, bf16[2,80,1920]{2,1,0:T(8,128)(2,1)}, u32[]{:S(2)}, u32[]{:S(2)}) %collective-permute-start.2) | collective-permute-done | bytes 614432 | tf_op jit(solution)/shard_map/ppermute | solution.py:22
  63.1 1.3 broadcast_select_fusion.3
  64.4 1.2 pad_maximum_fusion.5
  65.5 2.0 collective-permute-start.3
  69.7 127.4 %all_gather.7 = bf16[640,256]{1,0:T(8,128)(2,1)S(1)} all-gather(bf16[80,256]{1,0:T(8,128)(2,1)S(1)} %copy-done.15), channel_id=1, replica_groups=mesh['dp'=8,'tm'=4] {'dp'}, dimensions={0}, use_global_device_ids=true | all-gather | bytes 368640 | tf_op jit(solution)/shard_map/all_gather | solution.py:121
  197.5 1.6 broadcast_select_fusion.1
  199.1 1.7 pad_maximum_fusion.2
  200.8 6.2 reshape_reshape.3
  206.9 3.7 fusion.8
  210.7 1.5 collective-permute-start.4
  212.8 1.9 collective-permute-done.4
  215.2 1.2 broadcast_multiply_fusion
  216.4 10.2 %copy.31 = bf16[640,5760]{0,1:T(8,128)(2,1)} copy(bf16[640,5760]{1,0:T(8,128)(2,1)} %all-gather.2.cloned.1.call-done) | data formatting | bytes 14745600 | tf_op jit(solution)/shard_map/all_gather | solution.py:119
  226.6 15.7 %fusion.19 = f32[1024,640,9]{1,0,2:T(8,128)} fusion(bf16[1024,640,1]{1,0,2:T(8,128)(2,1)S(1)} %bitcast.161, bf16[640,9,640]{0,2,1:T(8,128)(2,1)} %bitcast.134), kind=kOutput, calls=%fused_computation.90 | convolution fusion | flops 7549747200 | bytes 32276480 | tf_op jit(solution)/shard_map/rq,ckq->rkc/dot_general | solution.py:142
  242.3 13.8 %slice_bitcast_fusion.8 = (f32[4,16,16,640]{3,2,1,0:T(8,128)}, f32[4,16,16,640]{3,2,1,0:T(8,128)S(1)}, f32[4,16,16,640]{3,2,1,0:T(8,128)S(1)}, f32[4,16,16,640]{...) fusion(f32[4,16,16,9,640]{4,2,1,0,3:T(8,128)} %bitcast.129), kind=kLoop, calls=%fused_computation.24 | loop fusion | bytes 47185920 | tf_op jit(solution)/shard_map/squeeze | solution.py:76
  256.2 4.2 pad_add_fusion
  261.0 0.8 copy-done.4
  261.8 3.8 multiply_multiply_fusion
  265.6 1.0 fusion.16
  266.6 3.0 pad_slice_fusion
  270.8 0.8 constant_dynamic-update-slice_fusion.4
  271.7 4.4 copy-done.14
  276.0 1.2 constant_dynamic-update-slice_fusion.3
  277.2 1.2 constant_dynamic-update-slice_fusion.2
  278.4 1.2 constant_dynamic-update-slice_fusion.1
  279.6 1.2 constant_dynamic-update-slice_fusion
  280.8 12.7 %fusion.3 = bf16[1024,640]{1,0:T(8,128)(2,1)S(1)} fusion(bf16[1024,9,640]{2,0,1:T(8,128)(2,1)} %constant_dynamic-update-slice_fusion, bf16[640,9,640]{0,2,1:T(8,128)(2,1)S(1)} %bitcast.137, f32[640]{0:T(1024)S(1)} %convolution_reduce_fusion), kind=kOutput, calls=%fused_computation.31 | convolution fusion | flops 7551057920 | bytes 20482560 | tf_op jit(solution)/shard_map/rkc,ckq->rq/dot_general | solution.py:106
  293.6 0.8 slice.149
  294.3 10.5 %collective-permute-start = (bf16[256,640]{1,0:T(8,128)(2,1)}, bf16[256,640]{1,0:T(8,128)(2,1)}, u32[]{:S(2)}, u32[]{:S(2)}) collective-permute-start(bf16[256,640]{1,0:T(8,128)(2,1)} %slice.149), channel_id=1, source_target_pairs={{0,1},{1,2},{2,3},{4,5},{5,6},{6,7},{8,9},{9,10},{10,11},{12,13},{... | collective-permute-start | bytes 983048 | tf_op jit(solution)/shard_map/ppermute | solution.py:36
  304.8 14.9 %fusion.20 = f32[640,9,640]{2,0,1:T(8,128)} fusion(bf16[1024,640,1]{1,0,2:T(8,128)(2,1)S(1)} %bitcast.162, bf16[1024,9,640]{2,0,1:T(8,128)(2,1)} %constant_dynamic-update-slice_fusion), kind=kOutput, calls=%fused_computation.91 | convolution fusion | flops 7549747200 | bytes 27852800 | tf_op jit(solution)/shard_map/rkc,rq->ckq/dot_general | solution.py:155
  319.7 15.2 %copy.42 = f32[640,5760]{1,0:T(8,128)} copy(f32[640,5760]{0,1:T(8,128)} %bitcast.130) | data formatting | bytes 29491200 | tf_op jit(solution)/shard_map/reshape | solution.py:163
  335.1 1.4 pad_maximum_fusion.4
  336.5 3.9 fusion.15
  340.4 5.9 copy.43
  346.3 15.2 %pad_maximum_fusion = f32[640,7936]{1,0:T(8,128)} fusion(f32[640,256]{1,0:T(8,128)S(1)} %copy-done.11, f32[640,1920]{1,0:T(8,128)} %copy.43, f32[640,5760]{1,0:T(8,128)} %copy.42), kind=kLoop, calls=%fused_computation | loop fusion | flops 10158080 | bytes 40632320 | tf_op jit(solution)/shard_map/concatenate | solution.py:161
  362.4 331.0 %reduce-scatter.2.cloned.1.call-done = f32[80,7936]{1,0:T(8,128)} async-done(((f32[640,7936]{1,0:T(8,128)}), f32[80,7936]{1,0:T(8,128)}) %reduce-scatter.2.cloned.1.call-update) | async-done | bytes 2539536 | tf_op jit(solution)/shard_map/reduce_scatter | solution.py:160
  693.5 4.7 fusion.2
  698.5 1.7 copy-done.5
  700.2 1.8 fusion.6
  702.1 1.1 copy.44
  703.2 50.7 %all-reduce.13.cloned.1.call-done = f32[80,7936]{1,0:T(8,128)} async-done(((f32[80,7936]{1,0:T(8,128)}), f32[80,7936]{1,0:T(8,128)}) %all-reduce.13.cloned.1.call-update) | async-done | bytes 2539536 | tf_op jit(solution)/shard_map/psum | solution.py:173
  754.0 2.9 slice.165
  756.8 1.9 slice.166
  758.8 1.5 slice.167
  (86 shorter events, 7.7 us)
Async XLA Ops:
  7.2 199.8 %copy-start = (bf16[1,2,16,16,640]{4,3,2,1,0:T(8,128)(2,1)S(1)}, bf16[1,2,16,16,640]{4,3,2,1,0:T(8,128)(2,1)}, u32[]{:S(2)}) copy-start(bf16[1,2,16,16,640]{4,3,2,1,0:T(8,128)(2,1)} %param.9) | copy-start | bytes 1966084
  7.2 209.2 %all-gather.2.cloned.1.call-start = ((), (), s32[]{:S(2)}) async-start(), calls=%async_computation.1 | async-start | bytes 8294400 | tf_op jit(solution)/shard_map/all_gather | solution.py:119
  7.9 685.6 %reduce-scatter.2.cloned.1.call-start = ((), (), s32[]{:S(2)}) async-start(), calls=%async_computation.2 | async-start | bytes 22855680 | tf_op jit(solution)/shard_map/reduce_scatter | solution.py:160
  8.0 10.5 %collective-permute-start.1 = (bf16[1,80,1920]{2,1,0:T(8,128)(2,1)}, bf16[1,80,1920]{2,1,0:T(8,128)(2,1)S(1)}, u32[]{:S(2)}, u32[]{:S(2)}) collective-permute-start(bf16[1,80,1920]{2,1,0:T(8,128)(2,1)} %bitcast.163), channel_id=1, source_target_pairs={{0,4},{4,0},{8,12},{12,8},{16,20},{20,16},{24,28},{28,24},{1,5},{5... | collective-permute-start | bytes 921608 | tf_op jit(solution)/shard_map/ppermute | solution.py:22
  19.5 0.7 copy-start.6
  20.3 47.2 %copy-start.1 = (bf16[1,4,16,16,640]{4,3,2,1,0:T(8,128)(2,1)S(1)}, bf16[1,4,16,16,640]{4,3,2,1,0:T(8,128)(2,1)}, u32[]{:S(2)}) copy-start(bf16[1,4,16,16,640]{4,3,2,1,0:T(8,128)(2,1)} %param.8) | copy-start | bytes 3932164
  20.3 42.8 %collective-permute-start.2 = (bf16[2,80,1920]{2,1,0:T(8,128)(2,1)S(1)}, bf16[2,80,1920]{2,1,0:T(8,128)(2,1)}, u32[]{:S(2)}, u32[]{:S(2)}) collective-permute-start(bf16[2,80,1920]{2,1,0:T(8,128)(2,1)S(1)} %pad_maximum_fusion.6), channel_id=1, source_target_pairs={{0,8},{4,12},{8,0},{12,4},{16,24},{20,28},{24,16},{28,20},{1,9},{5... | collective-permute-start | bytes 1843208 | tf_op jit(solution)/shard_map/ppermute | solution.py:22
  64.4 5.3 copy-start.15
  65.5 132.0 %collective-permute-start.3 = (bf16[4,80,1920]{2,1,0:T(8,128)(2,1)}, bf16[4,80,1920]{2,1,0:T(8,128)(2,1)}, u32[]{:S(2)}, u32[]{:S(2)}) collective-permute-start(bf16[4,80,1920]{2,1,0:T(8,128)(2,1)} %pad_maximum_fusion.5), channel_id=1, source_target_pairs={{0,16},{4,20},{8,24},{12,28},{16,0},{20,4},{24,8},{28,12},{1,17},{... | collective-permute-start | bytes 3686408 | tf_op jit(solution)/shard_map/ppermute | solution.py:22
  210.7 4.0 collective-permute-start.4
  215.2 11.4 %copy-start.12 = (bf16[4,256,640]{2,1,0:T(8,128)(2,1)}, bf16[4,256,640]{2,1,0:T(8,128)(2,1)S(1)}, u32[]{:S(2)}) copy-start(bf16[4,256,640]{2,1,0:T(8,128)(2,1)S(1)} %get-tuple-element.38) | copy-start | bytes 3932164
  256.1 4.3 copy-start.2
  256.1 4.8 copy-start.3
  256.2 5.6 copy-start.4
  270.8 10.0 %slice-start = ((s8[7372800]{0:T(1024)(128)(4,1)}), s8[4194304]{0:T(1024)(128)(4,1)S(1)}, s32[]{:S(2)}) async-start(s8[7372800]{0:T(1024)(128)(4,1)} %bitcast.135), calls=%async_computation.4 | async-start | bytes 8388608
  271.7 4.4 copy-start.14
  276.0 4.8 slice-start.1
  280.8 24.0 %copy-start.13 = (bf16[4,256,640]{2,1,0:T(8,128)(2,1)S(1)}, bf16[4,256,640]{2,1,0:T(8,128)(2,1)}, u32[]{:S(2)}) copy-start(bf16[4,256,640]{2,1,0:T(8,128)(2,1)} %copy-done.12) | copy-start | bytes 3932164
  294.3 40.7 %collective-permute-start = (bf16[256,640]{1,0:T(8,128)(2,1)}, bf16[256,640]{1,0:T(8,128)(2,1)}, u32[]{:S(2)}, u32[]{:S(2)}) collective-permute-start(bf16[256,640]{1,0:T(8,128)(2,1)} %slice.149), channel_id=1, source_target_pairs={{0,1},{1,2},{2,3},{4,5},{5,6},{6,7},{8,9},{9,10},{10,11},{12,13},{... | collective-permute-start | bytes 983048 | tf_op jit(solution)/shard_map/ppermute | solution.py:36
  335.0 5.3 copy-start.7
  335.0 5.3 copy-start.9
  340.4 5.9 copy-start.11
  361.5 392.4 %all-reduce.13.cloned.1.call-start = ((), (), s32[]{:S(2)}) async-start(), calls=%async_computation.3 | async-start | bytes 5079040 | tf_op jit(solution)/shard_map/psum | solution.py:173
  693.5 4.7 copy-start.8
  693.5 4.7 copy-start.10
  698.2 1.9 copy-start.5
Sparse Core Ops, SparseCore 0:
  10.2 168.7 all-gather.1
  361.7 331.7 reduce-scatter.1
  696.0 57.9 all-reduce.12
